TPU v7x, 32 devices: a whole 2x2x4 slice. The times are simulated.
32 devices in a mesh: ctx: 16 (over z, y, core), head: 2 (over x).
Axes of the slice: x: 2, y: 2, z: 4, core: 2. Of those that a mesh axis runs over, the one named last changes fastest.
Arguments:
- queries: bfloat16 [2048, 8192], P('ctx', 'head'), may hold values from -5.5 to 5.5
- keys: bfloat16 [2048, 1024], P('ctx', 'head'), may hold values from -5.5 to 5.5
- values: bfloat16 [2048, 1024], P('ctx', 'head'), may hold values from -6 to 6
- feature_weights: bfloat16 [64, 128, 64], P('head'), may hold values from -1 to 1
Outputs:
- attn_error: float32 [2048, 8192], P('ctx', 'head')
- loss: float32 [], replicated
- grad_w: float32 [64, 128, 64], P('head')
All inputs are finite; a program needn't handle non-finite values.
Results may differ from a plain program's by a relative error of at most 0.004.
Values may be sent and summed in bfloat16 or wider, within the bound.
No kernel may reach another device: no remote copies, remote signals or barrier semaphores. Data moves between devices by JAX's collectives and lax.ppermute only.
A program may use at most 192 MiB of HBM per device.

v0:
```python
import math
import jax
import jax.numpy as jnp
from jax import lax
from jax.sharding import PartitionSpec as P

HEAD_SIZE = 128
QUERY_HEADS = 64
KEY_VALUE_HEADS = 8
FM = 64
WIN = 64
phi_scale = 0.00390625
big_negative = -1e30
highest = lax.Precision.HIGHEST


def swapped(value, axis, distance):
    mask = 2**distance
    pairs = [(source, source ^ mask) for source in range(lax.axis_size(axis))]
    return lax.ppermute(value, axis, pairs)


def carried_in(value, axis, combine, identity):
    devices, here = (lax.axis_size(axis), lax.axis_index(axis))
    everything = jax.tree.map(
        lambda part, kind: lax.all_gather(part.astype(kind), axis),
        value,
        (jnp.bfloat16, jnp.bfloat16),
    )
    start = jax.tree.map(
        lambda part, zero: jnp.broadcast_to(jnp.asarray(zero, part.dtype), part.shape),
        value,
        identity,
    )

    def carried_step(k, before):
        reached = k < here
        new = combine(
            before, jax.tree.map(lambda part, own: part[k].astype(own.dtype), everything, value)
        )
        return jax.tree.map(lambda a, b: jnp.where(reached, a, b), new, before)

    return lax.fori_loop(0, devices, carried_step, start)


def prefix(value, axis, combine, identity):
    devices, here = (lax.axis_size(axis), lax.axis_index(axis))
    everything = jax.tree.map(
        lambda part, kind: lax.all_gather(part.astype(kind), axis),
        value,
        jax.tree.map(lambda a: jnp.bfloat16 if a.dtype == jnp.float32 else a.dtype, value),
    )
    start = jax.tree.map(
        lambda part, zero: jnp.broadcast_to(jnp.asarray(zero, part.dtype), part.shape),
        value,
        identity,
    )

    def prefix_step(k, before):
        at = devices - 1 - k
        reached = at > here
        new = combine(
            before, jax.tree.map(lambda part, own: part[at].astype(own.dtype), everything, value)
        )
        return jax.tree.map(lambda a, b: jnp.where(reached, a, b), new, before)

    return lax.fori_loop(0, devices, prefix_step, start)


def features(projection):
    return phi_scale * jnp.concatenate(
        [1.0 + jax.nn.elu(projection), 1.0 + jax.nn.elu(-projection)], axis=-1
    )


def feature_back(projection, grad_phi):
    half = projection.shape[-1]
    slope_plus = jnp.where(projection > 0, 1.0, jnp.exp(jnp.minimum(projection, 0.0)))
    slope_minus = jnp.where(projection < 0, 1.0, jnp.exp(jnp.minimum(-projection, 0.0)))
    return phi_scale * (grad_phi[..., :half] * slope_plus - grad_phi[..., half:] * slope_minus)


def add_pair(earlier, later):
    return (earlier[0] + later[0], earlier[1] + later[1])


def split_product(form, phi_part, data):
    upper = phi_part.astype(jnp.bfloat16)
    lower = (phi_part - upper.astype(jnp.float32)).astype(jnp.bfloat16)
    return jnp.einsum(form, upper, data, preferred_element_type=jnp.float32) + jnp.einsum(
        form, lower, data, preferred_element_type=jnp.float32
    )


def visit_partner(rows):
    for bit_index in range(lax.axis_size("ctx").bit_length() - 1):
        rows = swapped(rows, "ctx", bit_index)
    return rows


def return_partner(rows):
    for bit_index in range(lax.axis_size("ctx").bit_length() - 1):
        rows = swapped(rows.astype(jnp.bfloat16), "ctx", bit_index).astype(rows.dtype)
    return rows


def teacher_part(part, query_set, pos_set, key_block, value_block, key_pos, masked):
    scale_factor = 1.0 / math.sqrt(query_set.shape[-1])
    scores = (
        jnp.einsum("qgrd,kgd->grqk", query_set, key_block, preferred_element_type=jnp.float32)
        * scale_factor
    )
    if masked:
        causal = key_pos[None, :] <= pos_set[:, None]
        top = jnp.maximum(part[0], jnp.max(jnp.where(causal, scores, big_negative), axis=-1))
        weights = jnp.exp(jnp.where(causal, scores - top[..., None], big_negative))
    else:
        top = jnp.maximum(part[0], jnp.max(scores, axis=-1))
        weights = jnp.exp(scores - top[..., None])
    rescale = jnp.exp(part[0] - top)
    total = part[1] * rescale + jnp.sum(weights, axis=-1)
    mixed = part[2] * rescale[..., None] + jnp.einsum(
        "grqk,kgd->grqd",
        weights.astype(jnp.bfloat16),
        value_block,
        preferred_element_type=jnp.float32,
    )
    return (top, total, mixed)


def advance(part, row_set, key_block, value_block, key_pos, first):
    query_set, pos_set = row_set
    needed = first <= pos_set[-1]
    straddle = key_pos[-1] > pos_set[0]
    branch_index = jnp.where(needed, jnp.where(straddle, 2, 1), 0).astype(jnp.int32)
    return lax.switch(
        branch_index,
        [
            lambda current: current,
            lambda current: teacher_part(
                current, query_set, pos_set, key_block, value_block, key_pos, False
            ),
            lambda current: teacher_part(
                current, query_set, pos_set, key_block, value_block, key_pos, True
            ),
        ],
        part,
    )


def shards(queries, keys, values, feature_weights):
    local_rows = queries.shape[0]
    half_rows = local_rows // 2
    groups = keys.shape[1] // HEAD_SIZE
    group_ratio = QUERY_HEADS // KEY_VALUE_HEADS
    heads_here = groups * group_ratio
    ctx_count = lax.axis_size("ctx")
    ctx_place = lax.axis_index("ctx")
    own_start = ctx_place * local_rows
    query4 = queries.reshape(local_rows, groups, group_ratio, HEAD_SIZE)
    own_keys = keys.reshape(local_rows, groups, HEAD_SIZE)
    own_values = values.reshape(local_rows, groups, HEAD_SIZE)
    weight4 = feature_weights.reshape(groups, group_ratio, HEAD_SIZE, FM)
    scale = 1.0 / math.sqrt(HEAD_SIZE)
    query_pos = own_start + jnp.arange(local_rows, dtype=jnp.int32)
    tail_offsets = jnp.arange(WIN, dtype=jnp.int32)
    proj_own = jnp.einsum("kgd,grdf->grkf", own_keys, weight4, preferred_element_type=jnp.float32)
    first_set = (query4[:half_rows], query_pos[:half_rows])
    partner_start = (ctx_count - 1 - ctx_place) * local_rows
    visiting = visit_partner(query4[half_rows:])
    second_set = (visiting, partner_start + half_rows + jnp.arange(half_rows, dtype=jnp.int32))
    row_sets = (first_set, second_set)

    def add_tail(tails, key_block, value_block, key_pos):
        pick = (key_pos[None, :] == own_start - WIN + tail_offsets[:, None]).astype(jnp.bfloat16)
        return (
            tails[0]
            + jnp.einsum("wk,kgd->wgd", pick, key_block, preferred_element_type=jnp.float32),
            tails[1]
            + jnp.einsum("wk,kgd->wgd", pick, value_block, preferred_element_type=jnp.float32),
        )

    part_zero = (
        jnp.full((groups, group_ratio, half_rows), big_negative, jnp.float32),
        jnp.zeros((groups, group_ratio, half_rows), jnp.float32),
        jnp.zeros((groups, group_ratio, half_rows, HEAD_SIZE), jnp.float32),
    )
    tail_zero = (
        jnp.zeros((WIN, groups, HEAD_SIZE), jnp.float32),
        jnp.zeros((WIN, groups, HEAD_SIZE), jnp.float32),
    )
    state_zero = (
        jnp.zeros((groups, group_ratio, 2 * FM, HEAD_SIZE), jnp.float32),
        jnp.zeros((groups, group_ratio, 2 * FM), jnp.float32),
    )
    carry = ((part_zero, part_zero), tail_zero, ())
    key_piece = lax.all_gather(keys, "ctx", axis=0, tiled=True)
    value_piece = lax.all_gather(values, "ctx", axis=0, tiled=True)
    piece_rows = key_piece.shape[0]
    stride = math.gcd(piece_rows, local_rows)
    count = piece_rows // stride
    key_blocks = key_piece.reshape(count, stride, groups, HEAD_SIZE)
    value_blocks = value_piece.reshape(count, stride, groups, HEAD_SIZE)

    def fold_step(state, inputs):
        key_block, value_block, number = inputs
        first = number * stride
        key_pos = first + jnp.arange(stride, dtype=jnp.int32)
        parts_now, tails_now, states_now = state
        new_parts = (
            advance(parts_now[0], row_sets[0], key_block, value_block, key_pos, first),
            advance(parts_now[1], row_sets[1], key_block, value_block, key_pos, first),
        )
        earlier_block = first < own_start
        new_tails = lax.cond(
            earlier_block,
            lambda current: add_tail(current, key_block, value_block, key_pos),
            lambda current: current,
            tails_now,
        )
        return ((new_parts, new_tails, states_now), None)

    carry, unused = lax.scan(
        fold_step, carry, (key_blocks, value_blocks, jnp.arange(count, dtype=jnp.int32))
    )
    phi_own = features(proj_own)
    local_kv = split_product("grkf,kgd->grfd", phi_own, own_values)
    state_kv, state_norm = carried_in(
        (local_kv, jnp.sum(phi_own, axis=2)), "ctx", add_pair, state_zero
    )
    parts_done, tails_done = (carry[0], carry[1])
    teacher_first = parts_done[0][2] / parts_done[0][1][..., None]
    teacher_second = parts_done[1][2] / parts_done[1][1][..., None]
    teacher_second = return_partner(teacher_second)
    teacher = jnp.concatenate([teacher_first, teacher_second], axis=2)
    tail_key = tails_done[0].astype(jnp.bfloat16)
    tail_value = tails_done[1].astype(jnp.bfloat16)
    slab_key = jnp.concatenate([tail_key, own_keys], axis=0)
    slab_value = jnp.concatenate([tail_value, own_values], axis=0).astype(jnp.float32)
    slab_rows = WIN + local_rows
    slab_pos = own_start - WIN + jnp.arange(slab_rows, dtype=jnp.int32)
    is_tail = jnp.arange(slab_rows, dtype=jnp.int32) < WIN
    proj_tail = jnp.einsum("kgd,grdf->grkf", tail_key, weight4, preferred_element_type=jnp.float32)
    proj_slab = jnp.concatenate([proj_tail, proj_own], axis=2)
    phi_slab = features(proj_slab)
    proj_query = jnp.einsum("qgrd,grdf->grqf", query4, weight4, preferred_element_type=jnp.float32)
    phi_query = features(proj_query)
    scores = (
        jnp.einsum("qgrd,kgd->grqk", query4, slab_key, preferred_element_type=jnp.float32) * scale
    )
    window = (
        (slab_pos[None, :] >= query_pos[:, None] - WIN)
        & (slab_pos[None, :] <= query_pos[:, None])
        & (slab_pos[None, :] >= 0)
    )
    far = jnp.logical_not(is_tail)[None, :] & (slab_pos[None, :] < query_pos[:, None] - WIN)
    coefficient = far.astype(jnp.float32) - (window & is_tail[None, :]).astype(jnp.float32)
    window_top = jnp.max(jnp.where(window, scores, big_negative), axis=-1)
    local = jnp.exp(jnp.where(window, scores - window_top[..., None], big_negative))
    kernel = jnp.einsum("grqf,grkf->grqk", phi_query, phi_slab, precision=highest)
    mixed = local + coefficient * kernel
    numerator = jnp.einsum("grqk,kgd->grqd", mixed, slab_value, precision=highest) + jnp.einsum(
        "grqf,grfd->grqd", phi_query, state_kv, precision=highest
    )
    denominator = jnp.sum(mixed, axis=-1) + jnp.einsum(
        "grqf,grf->grq", phi_query, state_norm, precision=highest
    )
    student = numerator / denominator[..., None]
    error = student - teacher
    attn_error = jnp.transpose(error, (2, 0, 1, 3)).reshape(local_rows, heads_here * HEAD_SIZE)
    whole_rows = local_rows * ctx_count
    loss = lax.psum(jnp.sum(error * error), ("ctx", "head")) / (whole_rows * QUERY_HEADS)
    grad_out = 2.0 * error / denominator[..., None]
    grad_den = -jnp.sum(grad_out * student, axis=-1)
    later_kv = jnp.einsum("grqf,grqd->grfd", phi_query, grad_out, precision=highest)
    later_norm = jnp.einsum("grqf,grq->grf", phi_query, grad_den, precision=highest)
    suffix_kv, suffix_norm = prefix((later_kv, later_norm), "ctx", add_pair, state_zero)
    grad_lin = coefficient * (
        jnp.einsum("grqd,kgd->grqk", grad_out, slab_value, precision=highest) + grad_den[..., None]
    )
    grad_phi_query = (
        jnp.einsum("grqk,grkf->grqf", grad_lin, phi_slab, precision=highest)
        + jnp.einsum("grqd,grfd->grqf", grad_out, state_kv, precision=highest)
        + grad_den[..., None] * state_norm[:, :, None, :]
    )
    grad_phi_slab = jnp.einsum("grqk,grqf->grkf", grad_lin, phi_query, precision=highest)
    own_extra = (
        jnp.einsum("kgd,grfd->grkf", own_values.astype(jnp.float32), suffix_kv, precision=highest)
        + suffix_norm[:, :, None, :]
    )
    grad_phi_slab = grad_phi_slab + jnp.concatenate(
        [jnp.zeros((groups, group_ratio, WIN, 2 * FM), jnp.float32), own_extra], axis=2
    )
    grad_proj_query = feature_back(proj_query, grad_phi_query)
    grad_proj_slab = feature_back(proj_slab, grad_phi_slab)
    grad_local = jnp.einsum(
        "qgrd,grqf->grdf", query4.astype(jnp.float32), grad_proj_query, precision=highest
    ) + jnp.einsum(
        "kgd,grkf->grdf", slab_key.astype(jnp.float32), grad_proj_slab, precision=highest
    )
    grad_w = lax.psum(grad_local.reshape(heads_here, HEAD_SIZE, FM), "ctx")
    return (attn_error, loss, grad_w)


def solution(mesh):
    placed = (P("ctx", "head"), P("ctx", "head"), P("ctx", "head"), P("head", None, None))
    return jax.shard_map(
        shards,
        mesh=mesh,
        in_specs=placed,
        out_specs=(P("ctx", "head"), P(), P("head", None, None)),
        check_vma=False,
    )
```

profile of v0, /device:TPU:0, one launch (start us, length us, event | category | flops | bytes accessed | tf_op | source)
XLA Modules:
  0.0 783.3 jit_solution(9861084651910707477)
XLA Ops:
  10.8 3.3 fusion.72
  15.5 2.4 add_convert_fusion
  20.6 2.5 copy.204
  23.1 2.5 collective-permute-start.1
  25.6 4.3 fusion.116
  29.9 8.6 %collective-permute-done.1 = bf16[64,4,8,128]{3,2,1,0:T(8,128)(2,1)} collective-permute-done((bf16[64,4,8,128]{3,2,1,0:T(8,128)(2,1)}, bf16[64,4,8,128]{3,2,1,0:T(8,128)(2,1)}, u32[]{:S(2)}, u32[]{:S(2)}) %collective-permute-start.1) | collective-permute-done | bytes 524320 | tf_op jit(solution)/shard_map/ppermute | solution.py:20
  40.3 5.5 fusion.79
  45.8 13.8 %collective-permute-done.2 = bf16[64,4,8,128]{3,2,1,0:T(8,128)(2,1)} collective-permute-done((bf16[64,4,8,128]{3,2,1,0:T(8,128)(2,1)}, bf16[64,4,8,128]{3,2,1,0:T(8,128)(2,1)}, u32[]{:S(2)}, u32[]{:S(2)}) %collective-permute-start.2) | collective-permute-done | bytes 524320 | tf_op jit(solution)/shard_map/ppermute | solution.py:20
  59.6 2.4 collective-permute-start.3
  64.5 4.3 maximum_multiply_fusion.1
  68.9 20.4 %collective-permute-done.3 = bf16[64,4,8,128]{3,2,1,0:T(8,128)(2,1)} collective-permute-done((bf16[64,4,8,128]{3,2,1,0:T(8,128)(2,1)}, bf16[64,4,8,128]{3,2,1,0:T(8,128)(2,1)}, u32[]{:S(2)}, u32[]{:S(2)}) %collective-permute-start.3) | collective-permute-done | bytes 524320 | tf_op jit(solution)/shard_map/ppermute | solution.py:20
  91.4 4.4 reshape.276
  95.8 16.4 %all-gather.11.cloned.1.call-done = bf16[2048,512]{1,0:T(8,128)(2,1)} async-done(((bf16[128,512]{1,0:T(8,128)(2,1)}), bf16[2048,512]{1,0:T(8,128)(2,1)}) %all-gather.11.cloned.1.call-update) | async-done | bytes 2097168 | tf_op jit(solution)/shard_map/all_gather | solution.py:198
  112.2 4.0 reshape.277
  118.3 193.6 %while.59 = (s32[]{:T(128)}, f32[4,8,64]{2,1,0:T(8,128)S(1)}, f32[4,8,64]{2,1,0:T(8,128)S(1)}, f32[4,8,64,128]{3,2,1,0:T(8,128)S(1)}, f32[4,8,64]{2,1,0:T(8,128)...) while((s32[]{:T(128)}, f32[4,8,64]{2,1,0:T(8,128)S(1)}, ...), condition=%wide.region_17.18_spmd.clone, body=%wide.region_0.17_spmd.clone.sunk | while | flops 291086528 | bytes 14226523 | solution.py:223
  124.5 3.4 conditional.10
  129.8 2.5 conditional.9
  138.9 3.4 conditional.10
  150.8 3.4 conditional.10
  162.7 3.4 conditional.10
  174.7 3.4 conditional.10
  186.6 3.4 conditional.10
  198.5 3.4 conditional.10
  210.5 3.4 conditional.10
  222.4 3.4 conditional.10
  234.3 3.4 conditional.10
  246.3 3.4 conditional.10
  258.2 3.4 conditional.10
  270.1 3.4 conditional.10
  282.1 3.4 conditional.10
  294.0 3.4 conditional.10
  305.9 3.5 conditional.10
  313.0 3.5 collective-permute-start.4
  316.5 64.0 %all-gather.1 = bf16[64,8,128]{2,1,0:T(8,128)(2,1)} all-gather(bf16[4,8,128]{2,1,0:T(8,128)(2,1)S(1)} %fusion.143), channel_id=3, replica_groups=mesh['ctx'=16,'head'=2] {'ctx'}, dimensions={0}, use_global_device_ids=true | all-gather | bytes 139264 | tf_op jit(solution)/shard_map/all_gather | solution.py:26
  384.5 4.6 fusion.46
  389.1 4.7 fusion.109
  393.8 4.8 collective-permute-done.5
  400.9 11.1 %collective-permute-done.6 = bf16[4,8,64,128]{3,2,1,0:T(8,128)(2,1)S(1)} collective-permute-done((bf16[4,8,64,128]{3,2,1,0:T(8,128)(2,1)S(1)}, bf16[4,8,64,128]{3,2,1,0:T(8,128)(2,1)S(1)}, u32[]{:S(2)}, u32[]{:S(2)}) %collective-permute-start.6) | collective-permute-done | bytes 524320 | tf_op jit(solution)/shard_map/ppermute | solution.py:20
  413.3 5.2 fusion.122
  418.5 18.1 %collective-permute-done.7 = bf16[4,8,64,128]{3,2,1,0:T(8,128)(2,1)S(1)} collective-permute-done((bf16[4,8,64,128]{3,2,1,0:T(8,128)(2,1)S(1)}, bf16[4,8,64,128]{3,2,1,0:T(8,128)(2,1)S(1)}, u32[]{:S(2)}, u32[]{:S(2)}) %collective-permute-start.7) | collective-permute-done | bytes 524320 | tf_op jit(solution)/shard_map/ppermute | solution.py:20
  437.7 49.1 %while.60 = (s32[]{:T(128)}, f32[4,8,128,128]{3,2,1,0:T(8,128)S(1)}, f32[4,8,128]{2,1,0:T(8,128)S(1)}, s32[]{:T(128)}, bf16[16,4,8,128,128]{4,3,2,1,0:T(8,128)(2...) while((s32[]{:T(128)}, f32[4,8,128,128]{3,2,1,0:T(8,128)S(1)}, ...), condition=%wide.region_21.22_spmd.clone, body=%wide.region_20.21_spmd.clone.sunk | while | flops 2113540 | bytes 5283955 | solution.py:43
  486.7 5.7 fusion.150
  492.5 6.4 multiply_reduce_fusion
  500.2 4.6 convolution_convert_fusion
  505.4 3.6 fusion.151
  509.0 19.1 %all-gather.3 = bf16[64,8,128]{2,1,0:T(8,128)(2,1)S(1)} all-gather(bf16[4,8,128]{2,1,0:T(8,128)(2,1)S(1)} %convert_element_type.142), channel_id=5, replica_groups=mesh['ctx'=16,'head'=2] {'ctx'}, dimensions={0}, use_global_device_ids=true | all-gather | bytes 139264 | tf_op jit(solution)/shard_map/all_gather | solution.py:49
  528.0 3.2 fusion.121
  531.3 7.9 %fusion.68 = f32[4,8,128,128]{3,2,1,0:T(8,128)S(1)} fusion(f32[4,8,128,192]{2,3,1,0:T(8,128)S(1)} %fusion.121, f32[4,8,128]{2,1,0:T(8,128)S(1)} %neg.21, f32[128,192]{0,1:T(8,128)S(1)} %convert_subtract_fusion, f32[4,8,192,64]{3,2,1,0:T(8,128)S(1)} %copy-done.11, f32[4,8,192,64]{3,2,1,0:T(8,128)S(1)} %copy-done.9), kind=kOutput, calls=%fused_computation.116 | convolution fusion | flops 1211105280 | bytes 8503296 | tf_op jit(solution)/shard_map/grqk,grkf->grqf/dot_general | solution.py:282
  539.2 4.8 multiply_add_fusion.4
  544.1 4.5 fusion.83
  548.6 81.4 %all-gather.15.cloned.1.call-done = bf16[64,8,128,128]{3,2,1,0:T(8,128)(2,1)} async-done(((bf16[4,8,128,128]{3,2,1,0:T(8,128)(2,1)}), bf16[64,8,128,128]{3,2,1,0:T(8,128)(2,1)}) %all-gather.15.cloned.1.call-update) | async-done | bytes 16777232 | tf_op jit(solution)/shard_map/all_gather | solution.py:49
  630.0 38.6 %while.61 = (s32[]{:T(128)}, f32[4,8,128,128]{3,2,1,0:T(8,128)S(1)}, f32[4,8,128]{2,1,0:T(8,128)S(1)}, s32[]{:T(128)}, bf16[16,4,8,128,128]{4,3,2,1,0:T(8,128)(2...) while((s32[]{:T(128)}, ...), condition=%wide.region_27.28_spmd.clone, body=%wide.region_26.27_spmd.clone.sunk | while | flops 2113544 | bytes 5284017 | solution.py:67
  630.0 2.4 add_select_fusion.10
  634.8 2.4 add_select_fusion.10
  637.2 2.4 add_select_fusion.10
  642.1 2.4 add_select_fusion.10
  644.5 2.4 add_select_fusion.10
  649.3 2.4 add_select_fusion.10
  651.7 2.4 add_select_fusion.10
  656.5 2.4 add_select_fusion.10
  670.2 5.7 pad_add_fusion
  675.9 5.3 fusion.102
  681.2 39.0 %psum.14 = f32[]{:T(128)} all-reduce(f32[]{:T(128)} %get-tuple-element.673), channel_id=1, replica_groups=mesh['ctx'=16,'head'=2] {'ctx','head'}, use_global_device_ids=true, to_apply=%region_24.25 | all-reduce | flops 1 | bytes 8 | tf_op jit(solution)/shard_map/psum | solution.py:272
  724.6 48.3 %all-reduce.3.cloned.1.call-done = f32[32,128,64]{1,2,0:T(8,128)} async-done(((f32[32,128,64]{1,2,0:T(8,128)}), f32[32,128,64]{1,2,0:T(8,128)}) %all-reduce.3.cloned.1.call-update) | async-done | bytes 1048592 | tf_op jit(solution)/shard_map/psum | solution.py:301
  (451 shorter events, 225.4 us)
Async XLA Ops:
  7.2 3.6 copy-start
  7.2 84.2 %all-gather.9.cloned.1.call-start = ((), (), s32[]{:S(2)}) async-start(), calls=%async_computation | async-start | bytes 2228224 | tf_op jit(solution)/shard_map/all_gather | solution.py:197
  7.9 104.2 %all-gather.11.cloned.1.call-start = ((), (), s32[]{:S(2)}) async-start(), calls=%async_computation.1 | async-start | bytes 2228224 | tf_op jit(solution)/shard_map/all_gather | solution.py:198
  8.7 429.0 %all-gather.13.cloned.1.call-start = ((), (), s32[]{:S(2)}) async-start(), calls=%async_computation.3 | async-start | bytes 17825792 | tf_op jit(solution)/shard_map/all_gather | solution.py:26
  10.8 53.0 %copy-start.22 = (bf16[128,512]{0,1:T(8,128)(2,1)}, bf16[128,512]{0,1:T(8,128)(2,1)S(1)}, u32[]{:S(2)}) copy-start(bf16[128,512]{0,1:T(8,128)(2,1)S(1)} %copy.138) | copy-start | bytes 393220
  14.1 1.4 copy-start.13
  17.9 612.1 %all-gather.15.cloned.1.call-start = ((), (), s32[]{:S(2)}) async-start(), calls=%async_computation.4 | async-start | bytes 17825792 | tf_op jit(solution)/shard_map/all_gather | solution.py:49
  20.1 2.9 collective-permute-start
  23.1 15.4 %collective-permute-start.1 = (bf16[64,4,8,128]{3,2,1,0:T(8,128)(2,1)}, bf16[64,4,8,128]{3,2,1,0:T(8,128)(2,1)}, u32[]{:S(2)}, u32[]{:S(2)}) collective-permute-start(bf16[64,4,8,128]{3,2,1,0:T(8,128)(2,1)} %collective-permute-done), channel_id=1, source_target_pairs={{0,4},{2,6},{4,0},{6,2},{8,12},{10,14},{12,8},{14,10},{16,20},{18,... | collective-permute-start | bytes 1572872 | tf_op jit(solution)/shard_map/ppermute | solution.py:20
  29.9 16.0 %copy-start.28 = (u8[4,128,64]{2,1,0:T(8,128)(4,1)}, u8[4,128,64]{2,1,0:T(8,128)(4,1)S(1)}, u32[]{:S(2)}) copy-start(u8[4,128,64]{2,1,0:T(8,128)(4,1)S(1)} %get-tuple-element.671) | copy-start | bytes 98308
  38.5 21.1 %collective-permute-start.2 = (bf16[64,4,8,128]{3,2,1,0:T(8,128)(2,1)}, bf16[64,4,8,128]{3,2,1,0:T(8,128)(2,1)}, u32[]{:S(2)}, u32[]{:S(2)}) collective-permute-start(bf16[64,4,8,128]{3,2,1,0:T(8,128)(2,1)} %collective-permute-done.1), channel_id=1, source_target_pairs={{0,8},{2,10},{4,12},{6,14},{8,0},{10,2},{12,4},{14,6},{16,24},{18,... | collective-permute-start | bytes 1572872 | tf_op jit(solution)/shard_map/ppermute | solution.py:20
  40.3 21.7 %copy-start.14 = (f32[4,8,128,64]{3,2,1,0:T(8,128)S(1)}, f32[4,8,128,64]{3,2,1,0:T(8,128)}, u32[]{:S(2)}) copy-start(f32[4,8,128,64]{3,2,1,0:T(8,128)} %copy-done.13) | copy-start | bytes 3145732
  59.6 29.8 %collective-permute-start.3 = (bf16[64,4,8,128]{3,2,1,0:T(8,128)(2,1)}, bf16[64,4,8,128]{3,2,1,0:T(8,128)(2,1)}, u32[]{:S(2)}, u32[]{:S(2)}) collective-permute-start(bf16[64,4,8,128]{3,2,1,0:T(8,128)(2,1)} %collective-permute-done.2), channel_id=1, source_target_pairs={{0,16},{2,18},{4,20},{6,22},{8,24},{10,26},{12,28},{14,30},{16,0},... | collective-permute-start | bytes 1572872 | tf_op jit(solution)/shard_map/ppermute | solution.py:20
  313.0 71.4 %collective-permute-start.4 = (bf16[4,8,64,128]{3,2,1,0:T(8,128)(2,1)}, bf16[4,8,64,128]{3,2,1,0:T(8,128)(2,1)S(1)}, u32[]{:S(2)}, u32[]{:S(2)}) collective-permute-start(bf16[4,8,64,128]{3,2,1,0:T(8,128)(2,1)} %divide_convert_fusion), channel_id=1, source_target_pairs={{0,2},{2,0},{4,6},{6,4},{8,10},{10,8},{12,14},{14,12},{16,18},{18,... | collective-permute-start | bytes 1572872 | tf_op jit(solution)/shard_map/ppermute | solution.py:20
  384.3 4.7 copy-start.18
  384.4 14.2 %collective-permute-start.5 = (bf16[4,8,64,128]{3,2,1,0:T(8,128)(2,1)S(1)}, bf16[4,8,64,128]{3,2,1,0:T(8,128)(2,1)S(1)}, u32[]{:S(2)}, u32[]{:S(2)}) collective-permute-start(bf16[4,8,64,128]{3,2,1,0:T(8,128)(2,1)S(1)} %collective-permute-done.4), channel_id=1, source_target_pairs={{0,4},{2,6},{4,0},{6,2},{8,12},{10,14},{12,8},{14,10},{16,20},{18,... | collective-permute-start | bytes 1572872 | tf_op jit(solution)/shard_map/ppermute | solution.py:20
  384.4 4.6 copy-start.5
  389.0 4.7 copy-start.8
  389.0 4.7 copy-start.10
  389.1 9.6 %copy-start.20 = (bf16[16,8,32,128]{3,2,1,0:T(8,128)(2,1)S(1)}, bf16[16,8,32,128]{3,2,1,0:T(8,128)(2,1)}, u32[]{:S(2)}) copy-start(bf16[16,8,32,128]{3,2,1,0:T(8,128)(2,1)} %copy.204) | copy-start | bytes 3145732
  389.1 9.6 %copy-start.27 = (bf16[128,4,128]{2,0,1:T(8,128)(2,1)S(1)}, bf16[128,4,128]{2,0,1:T(8,128)(2,1)}, u32[]{:S(2)}) copy-start(bf16[128,4,128]{2,0,1:T(8,128)(2,1)} %copy.128) | copy-start | bytes 393220
  393.8 5.5 copy-start.17
  398.6 13.4 %collective-permute-start.6 = (bf16[4,8,64,128]{3,2,1,0:T(8,128)(2,1)S(1)}, bf16[4,8,64,128]{3,2,1,0:T(8,128)(2,1)S(1)}, u32[]{:S(2)}, u32[]{:S(2)}) collective-permute-start(bf16[4,8,64,128]{3,2,1,0:T(8,128)(2,1)S(1)} %collective-permute-done.5), channel_id=1, source_target_pairs={{0,8},{2,10},{4,12},{6,14},{8,0},{10,2},{12,4},{14,6},{16,24},{18,... | collective-permute-start | bytes 1572872 | tf_op jit(solution)/shard_map/ppermute | solution.py:20
  400.9 12.4 %copy-start.26 = (bf16[128,4,128]{2,0,1:T(8,128)(2,1)S(1)}, bf16[128,4,128]{2,0,1:T(8,128)(2,1)}, u32[]{:S(2)}) copy-start(bf16[128,4,128]{2,0,1:T(8,128)(2,1)} %copy.139) | copy-start | bytes 393220
  412.0 24.6 %collective-permute-start.7 = (bf16[4,8,64,128]{3,2,1,0:T(8,128)(2,1)S(1)}, bf16[4,8,64,128]{3,2,1,0:T(8,128)(2,1)S(1)}, u32[]{:S(2)}, u32[]{:S(2)}) collective-permute-start(bf16[4,8,64,128]{3,2,1,0:T(8,128)(2,1)S(1)} %collective-permute-done.6), channel_id=1, source_target_pairs={{0,16},{2,18},{4,20},{6,22},{8,24},{10,26},{12,28},{14,30},{16,0},... | collective-permute-start | bytes 1572872 | tf_op jit(solution)/shard_map/ppermute | solution.py:20
  413.3 24.3 %copy-start.2 = (f32[4,8,128,128]{3,2,1,0:T(8,128)S(1)}, f32[4,8,128,128]{3,2,1,0:T(8,128)}, u32[]{:S(2)}) copy-start(f32[4,8,128,128]{3,2,1,0:T(8,128)} %custom-call) | copy-start | bytes 6291460
  486.7 12.1 %copy-start.3 = (f32[4,8,128,128]{3,2,1,0:T(8,128)}, f32[4,8,128,128]{3,2,1,0:T(8,128)S(1)}, u32[]{:S(2)}) copy-start(f32[4,8,128,128]{3,2,1,0:T(8,128)S(1)} %get-tuple-element.496) | copy-start | bytes 6291460
  486.7 5.8 copy-start.6
  498.9 1.3 copy-start.15
  500.2 4.7 copy-start.30
  504.8 268.1 %all-reduce.3.cloned.1.call-start = ((), (), s32[]{:S(2)}) async-start(), calls=%async_computation.2 | async-start | bytes 2097152 | tf_op jit(solution)/shard_map/psum | solution.py:301
  505.3 25.9 %copy-start.11 = (f32[4,8,192,64]{3,2,1,0:T(8,128)S(1)}, f32[4,8,192,64]{3,2,1,0:T(8,128)}, u32[]{:S(2)}) copy-start(f32[4,8,192,64]{3,2,1,0:T(8,128)} %copy-done.10) | copy-start | bytes 4718596
  528.0 3.3 copy-start.9
  531.3 7.9 %copy-start.12 = (f32[4,8,128,192]{2,3,1,0:T(8,128)}, f32[4,8,128,192]{2,3,1,0:T(8,128)S(1)}, u32[]{:S(2)}) copy-start(f32[4,8,128,192]{2,3,1,0:T(8,128)S(1)} %fusion.121) | copy-start | bytes 9437188
  531.3 7.9 %copy-start.4 = (f32[4,8,128,128]{3,2,1,0:T(8,128)S(1)}, f32[4,8,128,128]{3,2,1,0:T(8,128)}, u32[]{:S(2)}) copy-start(f32[4,8,128,128]{3,2,1,0:T(8,128)} %copy-done.3) | copy-start | bytes 6291460
  531.3 7.9 %copy-start.16 = (f32[4,8,128,128]{3,2,1,0:T(8,128)S(1)}, f32[4,8,128,128]{3,2,1,0:T(8,128)}, u32[]{:S(2)}) copy-start(f32[4,8,128,128]{3,2,1,0:T(8,128)} %copy-done.15) | copy-start | bytes 6291460
  539.2 4.8 copy-start.21
  539.2 4.8 copy-start.24
  539.2 4.8 copy-start.29
  630.0 38.6 %copy-start.23 = (bf16[128,512]{0,1:T(8,128)(2,1)S(1)}, bf16[128,512]{0,1:T(8,128)(2,1)}, u32[]{:S(2)}) copy-start(bf16[128,512]{0,1:T(8,128)(2,1)} %copy-done.22) | copy-start | bytes 393220
  668.6 1.6 copy-start.7
  670.2 5.7 copy-start.19
  670.2 5.8 copy-start.25
  670.2 5.8 copy-start.31
  722.1 53.1 %copy-start.1 = (bf16[32,128,64]{1,2,0:T(8,128)(2,1)S(1)}, bf16[32,128,64]{1,2,0:T(8,128)(2,1)}, u32[]{:S(2)}) copy-start(bf16[32,128,64]{1,2,0:T(8,128)(2,1)} %param.21) | copy-start | bytes 1572868
Sparse Core Ops, SparseCore 0:
  10.2 45.6 all-gather.8
  58.0 54.1 all-gather.10
  114.3 125.7 all-gather.12
  505.0 124.9 all-gather.14
  681.3 91.5 all-reduce.2
where the time goes:
time: 796 us; the launch traced here: 783 us
  waiting for transfers between devices  224 us (28%)
  blocking collectives  122 us (15%)
  matrix products  120 us (15%)
  other arithmetic  120 us (15%)
  local copies, waits for them, and re-layouts  96.2 us (12%)
  loops' own time  72.7 us (9%)
  between operations  16.5 us (2%)
  starting transfers between devices  11 us (1%)
    all_gather x1, waiting for transfers between devices, prefix(): lax.all_gather(part.astype(kind), axis)  81.4 us
    ppermute x8, waiting for transfers between devices, swapped(): return lax.ppermute(value, axis, pairs)  76.8 us
    another operation x1, loops' own time, shards(): lax.scan(fold_step, carry, (key_blocks, value_blocks, jnp.arange(count, d...  70.5 us
    all_gather x1, blocking collectives, carried_in(): lax.all_gather(part.astype(kind), axis)  64 us
    select_n x32, other arithmetic, carried_step(): return jax.tree.map(lambda a, b: jnp.where(reached, a, b), new, before)  49 us
    psum x1, waiting for transfers between devices, shards(): grad_w = lax.psum(grad_local.reshape(heads_here, HEAD_SIZE, FM), 'ctx')  48.3 us
    psum x1, blocking collectives, shards(): lax.psum(jnp.sum(error * error), ('ctx', 'head'))  39 us
    dynamic_slice x64, local copies, waits for them, and re-layouts, shards(): lax.scan(fold_step, carry, (key_blocks, value_blocks, jnp.arange(count, d...  38.7 us
  transfers between devices with their start and end apart: 13, of which 9 were waited for; matrix products, arithmetic and copies ran while one was open for 28% of the time, Pallas kernels for 0%

commit v1 on v0

--- a/solution.py
+++ b/solution.py
@@ -194,8 +194,11 @@
         jnp.zeros((groups, group_ratio, 2 * FM), jnp.float32),
     )
     carry = ((part_zero, part_zero), tail_zero, ())
-    key_piece = lax.all_gather(keys, "ctx", axis=0, tiled=True)
-    value_piece = lax.all_gather(values, "ctx", axis=0, tiled=True)
+    key_piece, value_piece = jnp.split(
+        lax.all_gather(jnp.concatenate([keys, values], axis=1), "ctx", axis=0, tiled=True),
+        [keys.shape[1]],
+        axis=1,
+    )
     piece_rows = key_piece.shape[0]
     stride = math.gcd(piece_rows, local_rows)
     count = piece_rows // stride

time: 796 us -> 825 us (1.036)
  local copies, waits for them, and re-layouts: 96.2 us -> 113 us
  waiting for transfers between devices: 224 us -> 238 us
    ppermute x8, waiting for transfers between devices: 76.8 us -> 108 us  [swapped(): return lax.ppermute(value, axis, pairs)]
    all_gather x2 -> x1, waiting for transfers between devices: 16.4 us -> 0.01 us  [shards(): lax.all_gather(jnp.concatenate([keys, values], axis=1), 'ctx', axis=0, ti...]
    reshape x1, local copies, waits for them, and re-layouts: 4.4 us -> 16.5 us  [shards(): key_blocks = key_piece.reshape(count, stride, groups, HEAD_SIZE)]
  transfers between devices with their start and end apart: 13 -> 12, of which waited for: 9 -> 8; matrix products, arithmetic and copies ran while one was open for 28% -> 29% of each run, Pallas kernels for 0% -> 0%
where the time goes in v1:
time: 825 us; the launch traced here: 812 us
  waiting for transfers between devices  238 us (29%)
  other arithmetic  122 us (15%)
  blocking collectives  122 us (15%)
  matrix products  120 us (15%)
  local copies, waits for them, and re-layouts  113 us (14%)
  loops' own time  72.1 us (9%)
  between operations  16.5 us (2%)
  starting transfers between devices  8.31 us (1%)
    ppermute x8, waiting for transfers between devices, swapped(): return lax.ppermute(value, axis, pairs)  108 us
    all_gather x1, waiting for transfers between devices, prefix(): lax.all_gather(part.astype(kind), axis)  81.3 us
    another operation x1, loops' own time, shards(): lax.scan(fold_step, carry, (key_blocks, value_blocks, jnp.arange(count, d...  70 us
    all_gather x1, blocking collectives, carried_in(): lax.all_gather(part.astype(kind), axis)  64.2 us
    select_n x32, other arithmetic, carried_step(): return jax.tree.map(lambda a, b: jnp.where(reached, a, b), new, before)  49 us
    psum x1, waiting for transfers between devices, shards(): grad_w = lax.psum(grad_local.reshape(heads_here, HEAD_SIZE, FM), 'ctx')  48.3 us
    psum x1, blocking collectives, shards(): lax.psum(jnp.sum(error * error), ('ctx', 'head'))  39 us
    select_n x32, other arithmetic, prefix_step(): return jax.tree.map(lambda a, b: jnp.where(reached, a, b), new, before)  38 us
  transfers between devices with their start and end apart: 12, of which 8 were waited for; matrix products, arithmetic and copies ran while one was open for 29% of the time, Pallas kernels for 0%

profile of v1, /device:TPU:0, one launch (start us, length us, event | category | flops | bytes accessed | tf_op | source)
XLA Modules:
  0.0 812.5 jit_solution(16124239268378740649)
XLA Ops:
  11.1 3.3 fusion.72
  15.8 2.4 add_convert_fusion
  20.9 2.5 copy.204
  23.4 2.5 collective-permute-start.1
  25.9 4.3 fusion.116
  30.2 8.6 %collective-permute-done.1 = bf16[64,4,8,128]{3,2,1,0:T(8,128)(2,1)} collective-permute-done((bf16[64,4,8,128]{3,2,1,0:T(8,128)(2,1)}, bf16[64,4,8,128]{3,2,1,0:T(8,128)(2,1)}, u32[]{:S(2)}, u32[]{:S(2)}) %collective-permute-start.1) | collective-permute-done | bytes 524320 | tf_op jit(solution)/shard_map/ppermute | solution.py:20
  40.6 5.5 fusion.79
  46.2 23.6 %collective-permute-done.2 = bf16[64,4,8,128]{3,2,1,0:T(8,128)(2,1)} collective-permute-done((bf16[64,4,8,128]{3,2,1,0:T(8,128)(2,1)}, bf16[64,4,8,128]{3,2,1,0:T(8,128)(2,1)}, u32[]{:S(2)}, u32[]{:S(2)}) %collective-permute-start.2) | collective-permute-done | bytes 524320 | tf_op jit(solution)/shard_map/ppermute | solution.py:20
  72.8 4.2 maximum_multiply_fusion.1
  77.1 42.0 %collective-permute-done.3 = bf16[64,4,8,128]{3,2,1,0:T(8,128)(2,1)} collective-permute-done((bf16[64,4,8,128]{3,2,1,0:T(8,128)(2,1)}, bf16[64,4,8,128]{3,2,1,0:T(8,128)(2,1)}, u32[]{:S(2)}, u32[]{:S(2)}) %collective-permute-start.3) | collective-permute-done | bytes 524320 | tf_op jit(solution)/shard_map/ppermute | solution.py:20
  121.2 4.6 fusion.148
  125.7 16.5 %reshape.276 = bf16[16,128,4,128]{3,2,1,0:T(4,128)(2,1)} reshape(bf16[2048,512]{1,0:T(8,128)(2,1)} %get-tuple-element.759) | data formatting | bytes 4194304 | tf_op jit(solution)/shard_map/reshape | solution.py:205
  142.2 4.0 reshape.277
  148.3 193.1 %while.59 = (s32[]{:T(128)}, f32[4,8,64]{2,1,0:T(8,128)S(1)}, f32[4,8,64]{2,1,0:T(8,128)S(1)}, f32[4,8,64,128]{3,2,1,0:T(8,128)S(1)}, f32[4,8,64]{2,1,0:T(8,128)...) while((s32[]{:T(128)}, f32[4,8,64]{2,1,0:T(8,128)S(1)}, ...), condition=%wide.region_17.18_spmd.clone, body=%wide.region_0.17_spmd.clone.sunk | while | flops 291086528 | bytes 14226523 | solution.py:226
  154.4 3.4 conditional.10
  159.7 2.5 conditional.9
  168.7 3.4 conditional.10
  180.6 3.4 conditional.10
  192.5 3.5 conditional.10
  204.5 3.4 conditional.10
  216.4 3.4 conditional.10
  228.3 3.4 conditional.10
  240.2 3.4 conditional.10
  252.1 3.4 conditional.10
  264.0 3.4 conditional.10
  275.9 3.4 conditional.10
  287.8 3.4 conditional.10
  299.7 3.4 conditional.10
  311.6 3.4 conditional.10
  323.5 3.4 conditional.10
  335.4 3.5 conditional.10
  342.5 2.9 collective-permute-start.4
  345.4 64.2 %all-gather.1 = bf16[64,8,128]{2,1,0:T(8,128)(2,1)} all-gather(bf16[4,8,128]{2,1,0:T(8,128)(2,1)S(1)} %fusion.143), channel_id=3, replica_groups=mesh['ctx'=16,'head'=2] {'ctx'}, dimensions={0}, use_global_device_ids=true | all-gather | bytes 139264 | tf_op jit(solution)/shard_map/all_gather | solution.py:26
  413.6 4.6 fusion.46
  418.2 4.7 fusion.109
  422.9 4.8 collective-permute-done.5
  430.1 11.1 %collective-permute-done.6 = bf16[4,8,64,128]{3,2,1,0:T(8,128)(2,1)S(1)} collective-permute-done((bf16[4,8,64,128]{3,2,1,0:T(8,128)(2,1)S(1)}, bf16[4,8,64,128]{3,2,1,0:T(8,128)(2,1)S(1)}, u32[]{:S(2)}, u32[]{:S(2)}) %collective-permute-start.6) | collective-permute-done | bytes 524320 | tf_op jit(solution)/shard_map/ppermute | solution.py:20
  442.5 5.2 fusion.122
  447.7 18.1 %collective-permute-done.7 = bf16[4,8,64,128]{3,2,1,0:T(8,128)(2,1)S(1)} collective-permute-done((bf16[4,8,64,128]{3,2,1,0:T(8,128)(2,1)S(1)}, bf16[4,8,64,128]{3,2,1,0:T(8,128)(2,1)S(1)}, u32[]{:S(2)}, u32[]{:S(2)}) %collective-permute-start.7) | collective-permute-done | bytes 524320 | tf_op jit(solution)/shard_map/ppermute | solution.py:20
  466.8 49.1 %while.60 = (s32[]{:T(128)}, f32[4,8,128,128]{3,2,1,0:T(8,128)S(1)}, f32[4,8,128]{2,1,0:T(8,128)S(1)}, s32[]{:T(128)}, bf16[16,4,8,128,128]{4,3,2,1,0:T(8,128)(2...) while((s32[]{:T(128)}, f32[4,8,128,128]{3,2,1,0:T(8,128)S(1)}, ...), condition=%wide.region_21.22_spmd.clone, body=%wide.region_20.21_spmd.clone.sunk | while | flops 2113540 | bytes 5283955 | solution.py:43
  515.9 5.7 fusion.151
  521.7 6.4 multiply_reduce_fusion
  529.3 4.6 convolution_convert_fusion
  534.5 3.6 fusion.152
  538.1 19.2 %all-gather.3 = bf16[64,8,128]{2,1,0:T(8,128)(2,1)S(1)} all-gather(bf16[4,8,128]{2,1,0:T(8,128)(2,1)S(1)} %convert_element_type.142), channel_id=5, replica_groups=mesh['ctx'=16,'head'=2] {'ctx'}, dimensions={0}, use_global_device_ids=true | all-gather | bytes 139264 | tf_op jit(solution)/shard_map/all_gather | solution.py:49
  557.3 3.2 fusion.121
  560.6 7.9 fusion.68
  568.5 4.8 multiply_add_fusion.4
  573.3 4.5 fusion.83
  577.8 81.3 %all-gather.12.cloned.1.call-done = bf16[64,8,128,128]{3,2,1,0:T(8,128)(2,1)} async-done(((bf16[4,8,128,128]{3,2,1,0:T(8,128)(2,1)}), bf16[64,8,128,128]{3,2,1,0:T(8,128)(2,1)}) %all-gather.12.cloned.1.call-update) | async-done | bytes 16777232 | tf_op jit(solution)/shard_map/all_gather | solution.py:49
  659.2 38.6 %while.61 = (s32[]{:T(128)}, f32[4,8,128,128]{3,2,1,0:T(8,128)S(1)}, f32[4,8,128]{2,1,0:T(8,128)S(1)}, s32[]{:T(128)}, bf16[16,4,8,128,128]{4,3,2,1,0:T(8,128)(2...) while((s32[]{:T(128)}, ...), condition=%wide.region_27.28_spmd.clone, body=%wide.region_26.27_spmd.clone.sunk | while | flops 2113544 | bytes 5284017 | solution.py:67
  659.2 2.4 add_select_fusion.10
  664.0 2.4 add_select_fusion.10
  666.4 2.4 add_select_fusion.10
  671.2 2.4 add_select_fusion.10
  673.7 2.4 add_select_fusion.10
  678.5 2.4 add_select_fusion.10
  680.9 2.4 add_select_fusion.10
  685.7 2.4 add_select_fusion.10
  688.1 2.4 add_select_fusion.10
  699.4 5.7 pad_add_fusion
  705.1 5.3 fusion.102
  710.4 39.0 %psum.14 = f32[]{:T(128)} all-reduce(f32[]{:T(128)} %get-tuple-element.673), channel_id=1, replica_groups=mesh['ctx'=16,'head'=2] {'ctx','head'}, use_global_device_ids=true, to_apply=%region_24.25 | all-reduce | flops 1 | bytes 8 | tf_op jit(solution)/shard_map/psum | solution.py:275
  753.8 48.3 %all-reduce.3.cloned.1.call-done = f32[32,128,64]{1,2,0:T(8,128)} async-done(((f32[32,128,64]{1,2,0:T(8,128)}), f32[32,128,64]{1,2,0:T(8,128)}) %all-reduce.3.cloned.1.call-update) | async-done | bytes 1048592 | tf_op jit(solution)/shard_map/psum | solution.py:304
  (450 shorter events, 223.9 us)
Async XLA Ops:
  7.2 4.0 copy-start
  7.2 114.0 %all-gather.8.cloned.1.call-start = ((), (), s32[]{:S(2)}) async-start(), calls=%async_computation | async-start | bytes 4456448 | tf_op jit(solution)/shard_map/all_gather | solution.py:198
  9.0 457.8 %all-gather.10.cloned.1.call-start = ((), (), s32[]{:S(2)}) async-start(), calls=%async_computation.2 | async-start | bytes 17825792 | tf_op jit(solution)/shard_map/all_gather | solution.py:26
  11.1 60.9 %copy-start.22 = (bf16[128,512]{0,1:T(8,128)(2,1)}, bf16[128,512]{0,1:T(8,128)(2,1)S(1)}, u32[]{:S(2)}) copy-start(bf16[128,512]{0,1:T(8,128)(2,1)S(1)} %copy.138) | copy-start | bytes 393220
  14.4 1.4 copy-start.13
  18.2 640.9 %all-gather.12.cloned.1.call-start = ((), (), s32[]{:S(2)}) async-start(), calls=%async_computation.3 | async-start | bytes 17825792 | tf_op jit(solution)/shard_map/all_gather | solution.py:49
  20.5 3.0 collective-permute-start
  23.4 15.4 %collective-permute-start.1 = (bf16[64,4,8,128]{3,2,1,0:T(8,128)(2,1)}, bf16[64,4,8,128]{3,2,1,0:T(8,128)(2,1)}, u32[]{:S(2)}, u32[]{:S(2)}) collective-permute-start(bf16[64,4,8,128]{3,2,1,0:T(8,128)(2,1)} %collective-permute-done), channel_id=1, source_target_pairs={{0,4},{2,6},{4,0},{6,2},{8,12},{10,14},{12,8},{14,10},{16,20},{18,... | collective-permute-start | bytes 1572872 | tf_op jit(solution)/shard_map/ppermute | solution.py:20
  30.2 16.0 %copy-start.28 = (u8[4,128,64]{2,1,0:T(8,128)(4,1)}, u8[4,128,64]{2,1,0:T(8,128)(4,1)S(1)}, u32[]{:S(2)}) copy-start(u8[4,128,64]{2,1,0:T(8,128)(4,1)S(1)} %get-tuple-element.671) | copy-start | bytes 98308
  38.8 31.0 %collective-permute-start.2 = (bf16[64,4,8,128]{3,2,1,0:T(8,128)(2,1)}, bf16[64,4,8,128]{3,2,1,0:T(8,128)(2,1)}, u32[]{:S(2)}, u32[]{:S(2)}) collective-permute-start(bf16[64,4,8,128]{3,2,1,0:T(8,128)(2,1)} %collective-permute-done.1), channel_id=1, source_target_pairs={{0,8},{2,10},{4,12},{6,14},{8,0},{10,2},{12,4},{14,6},{16,24},{18,... | collective-permute-start | bytes 1572872 | tf_op jit(solution)/shard_map/ppermute | solution.py:20
  40.6 29.6 %copy-start.14 = (f32[4,8,128,64]{3,2,1,0:T(8,128)S(1)}, f32[4,8,128,64]{3,2,1,0:T(8,128)}, u32[]{:S(2)}) copy-start(f32[4,8,128,64]{3,2,1,0:T(8,128)} %copy-done.13) | copy-start | bytes 3145732
  69.8 49.3 %collective-permute-start.3 = (bf16[64,4,8,128]{3,2,1,0:T(8,128)(2,1)}, bf16[64,4,8,128]{3,2,1,0:T(8,128)(2,1)}, u32[]{:S(2)}, u32[]{:S(2)}) collective-permute-start(bf16[64,4,8,128]{3,2,1,0:T(8,128)(2,1)} %collective-permute-done.2), channel_id=1, source_target_pairs={{0,16},{2,18},{4,20},{6,22},{8,24},{10,26},{12,28},{14,30},{16,0},... | collective-permute-start | bytes 1572872 | tf_op jit(solution)/shard_map/ppermute | solution.py:20
  342.5 71.0 %collective-permute-start.4 = (bf16[4,8,64,128]{3,2,1,0:T(8,128)(2,1)}, bf16[4,8,64,128]{3,2,1,0:T(8,128)(2,1)S(1)}, u32[]{:S(2)}, u32[]{:S(2)}) collective-permute-start(bf16[4,8,64,128]{3,2,1,0:T(8,128)(2,1)} %divide_convert_fusion), channel_id=1, source_target_pairs={{0,2},{2,0},{4,6},{6,4},{8,10},{10,8},{12,14},{14,12},{16,18},{18,... | collective-permute-start | bytes 1572872 | tf_op jit(solution)/shard_map/ppermute | solution.py:20
  413.5 4.7 copy-start.18
  413.5 14.2 %collective-permute-start.5 = (bf16[4,8,64,128]{3,2,1,0:T(8,128)(2,1)S(1)}, bf16[4,8,64,128]{3,2,1,0:T(8,128)(2,1)S(1)}, u32[]{:S(2)}, u32[]{:S(2)}) collective-permute-start(bf16[4,8,64,128]{3,2,1,0:T(8,128)(2,1)S(1)} %collective-permute-done.4), channel_id=1, source_target_pairs={{0,4},{2,6},{4,0},{6,2},{8,12},{10,14},{12,8},{14,10},{16,20},{18,... | collective-permute-start | bytes 1572872 | tf_op jit(solution)/shard_map/ppermute | solution.py:20
  413.6 4.6 copy-start.5
  418.2 4.7 copy-start.8
  418.2 4.7 copy-start.10
  418.2 9.6 %copy-start.20 = (bf16[16,8,32,128]{3,2,1,0:T(8,128)(2,1)S(1)}, bf16[16,8,32,128]{3,2,1,0:T(8,128)(2,1)}, u32[]{:S(2)}) copy-start(bf16[16,8,32,128]{3,2,1,0:T(8,128)(2,1)} %copy.204) | copy-start | bytes 3145732
  418.2 9.5 %copy-start.27 = (bf16[128,4,128]{2,0,1:T(8,128)(2,1)S(1)}, bf16[128,4,128]{2,0,1:T(8,128)(2,1)}, u32[]{:S(2)}) copy-start(bf16[128,4,128]{2,0,1:T(8,128)(2,1)} %copy.128) | copy-start | bytes 393220
  422.9 5.5 copy-start.17
  427.8 13.4 %collective-permute-start.6 = (bf16[4,8,64,128]{3,2,1,0:T(8,128)(2,1)S(1)}, bf16[4,8,64,128]{3,2,1,0:T(8,128)(2,1)S(1)}, u32[]{:S(2)}, u32[]{:S(2)}) collective-permute-start(bf16[4,8,64,128]{3,2,1,0:T(8,128)(2,1)S(1)} %collective-permute-done.5), channel_id=1, source_target_pairs={{0,8},{2,10},{4,12},{6,14},{8,0},{10,2},{12,4},{14,6},{16,24},{18,... | collective-permute-start | bytes 1572872 | tf_op jit(solution)/shard_map/ppermute | solution.py:20
  430.1 12.4 %copy-start.26 = (bf16[128,4,128]{2,0,1:T(8,128)(2,1)S(1)}, bf16[128,4,128]{2,0,1:T(8,128)(2,1)}, u32[]{:S(2)}) copy-start(bf16[128,4,128]{2,0,1:T(8,128)(2,1)} %copy.139) | copy-start | bytes 393220
  441.1 24.6 %collective-permute-start.7 = (bf16[4,8,64,128]{3,2,1,0:T(8,128)(2,1)S(1)}, bf16[4,8,64,128]{3,2,1,0:T(8,128)(2,1)S(1)}, u32[]{:S(2)}, u32[]{:S(2)}) collective-permute-start(bf16[4,8,64,128]{3,2,1,0:T(8,128)(2,1)S(1)} %collective-permute-done.6), channel_id=1, source_target_pairs={{0,16},{2,18},{4,20},{6,22},{8,24},{10,26},{12,28},{14,30},{16,0},... | collective-permute-start | bytes 1572872 | tf_op jit(solution)/shard_map/ppermute | solution.py:20
  442.5 24.3 %copy-start.2 = (f32[4,8,128,128]{3,2,1,0:T(8,128)S(1)}, f32[4,8,128,128]{3,2,1,0:T(8,128)}, u32[]{:S(2)}) copy-start(f32[4,8,128,128]{3,2,1,0:T(8,128)} %custom-call) | copy-start | bytes 6291460
  515.9 12.1 %copy-start.3 = (f32[4,8,128,128]{3,2,1,0:T(8,128)}, f32[4,8,128,128]{3,2,1,0:T(8,128)S(1)}, u32[]{:S(2)}) copy-start(f32[4,8,128,128]{3,2,1,0:T(8,128)S(1)} %get-tuple-element.496) | copy-start | bytes 6291460
  515.9 5.8 copy-start.6
  528.0 1.3 copy-start.15
  529.3 4.7 copy-start.30
  534.0 268.1 %all-reduce.3.cloned.1.call-start = ((), (), s32[]{:S(2)}) async-start(), calls=%async_computation.1 | async-start | bytes 2097152 | tf_op jit(solution)/shard_map/psum | solution.py:304
  534.5 26.0 %copy-start.11 = (f32[4,8,192,64]{3,2,1,0:T(8,128)S(1)}, f32[4,8,192,64]{3,2,1,0:T(8,128)}, u32[]{:S(2)}) copy-start(f32[4,8,192,64]{3,2,1,0:T(8,128)} %copy-done.10) | copy-start | bytes 4718596
  557.3 3.3 copy-start.9
  560.5 7.9 copy-start.12
  560.5 7.9 copy-start.4
  560.5 7.9 copy-start.16
  568.5 4.8 copy-start.21
  568.5 4.8 copy-start.24
  568.5 4.8 copy-start.29
  659.2 38.6 %copy-start.23 = (bf16[128,512]{0,1:T(8,128)(2,1)S(1)}, bf16[128,512]{0,1:T(8,128)(2,1)}, u32[]{:S(2)}) copy-start(bf16[128,512]{0,1:T(8,128)(2,1)} %copy-done.22) | copy-start | bytes 393220
  697.8 1.6 copy-start.7
  699.3 5.7 copy-start.19
  699.3 5.8 copy-start.25
  699.3 5.8 copy-start.31
  751.3 53.1 %copy-start.1 = (bf16[32,128,64]{1,2,0:T(8,128)(2,1)S(1)}, bf16[32,128,64]{1,2,0:T(8,128)(2,1)}, u32[]{:S(2)}) copy-start(bf16[32,128,64]{1,2,0:T(8,128)(2,1)} %param.21) | copy-start | bytes 1572868
Sparse Core Ops, SparseCore 0:
  10.2 60.3 all-gather.7
  72.7 137.4 all-gather.9
  534.1 125.0 all-gather.11
  710.5 91.5 all-reduce.2
